TPU v7x, 32 devices: a whole 2x2x4 slice. The times are simulated.
32 devices in a mesh: dp: 8 (over y, x, core), mp: 4 (over z).
Axes of the slice: x: 2, y: 2, z: 4, core: 2. Of those that a mesh axis runs over, the one named last changes fastest.
Arguments:
- patches: bfloat16 [8192, 1024], P(('dp', 'mp')), as said below
- scene_ids: int32 [8192], P(('dp', 'mp')), may hold values from 0 to 7, as said below
- owner_ids: int32 [8192], P(('dp', 'mp')), may hold values from 0 to 7, as said below
- fill_slot: int32 [32768], P(('dp', 'mp')), may hold values from -1 to 511, as said below
- norm1_gain: float32 [1024], replicated, may hold values from 0.1 to 1.9
- norm1_bias: float32 [1024], replicated, may hold values from -1.75 to 1.75
- qkv_weight: bfloat16 [1024, 3, 1024], P(None, None, 'mp'), may hold values from -0.25 to 0.25
- qv_bias: float32 [2, 1024], P(None, 'mp'), may hold values from -3 to 3
- out_weight: bfloat16 [1024, 1024], P('mp'), may hold values from -1.5 to 1.5
- out_bias: float32 [1024], replicated, may hold values from -1.75 to 1.75
- norm2_gain: float32 [1024], replicated, may hold values from 0.1 to 1.9
- norm2_bias: float32 [1024], replicated, may hold values from -1.75 to 1.75
- up_weight: bfloat16 [1024, 4096], P(None, 'mp'), may hold values from -0.1875 to 0.1875
- up_bias: bfloat16 [4096], P('mp'), may hold values from -3 to 3
- down_weight: bfloat16 [4096, 1024], P('mp'), may hold values from -0.125 to 0.125
- down_bias: float32 [1024], replicated, may hold values from -1.75 to 1.75
- dec_weight: bfloat16 [1024, 512], replicated, may hold values from -0.1875 to 0.1875
- dec_bias: float32 [512], replicated, may hold values from -1.75 to 1.75
- mask_token: float32 [512], replicated, may hold values from -6 to 6
- positions: bfloat16 [32768, 512], P(('dp', 'mp')), may hold values from -6 to 6
- cotangent: bfloat16 [32768, 512], P(('dp', 'mp')), may hold values from -6 to 6
Outputs:
- decoder_in: bfloat16 [32768, 512], P(('dp', 'mp'))
- grad_patches: float32 [8192, 1024], P(('dp', 'mp'))
- grad_norm1_gain: float32 [1024], replicated
- grad_norm1_bias: float32 [1024], replicated
- grad_qkv_weight: float32 [1024, 3, 1024], P(None, None, 'mp')
- grad_qv_bias: float32 [2, 1024], P(None, 'mp')
- grad_out_weight: float32 [1024, 1024], P('mp')
- grad_out_bias: float32 [1024], replicated
- grad_norm2_gain: float32 [1024], replicated
- grad_norm2_bias: float32 [1024], replicated
- grad_up_weight: float32 [1024, 4096], P(None, 'mp')
- grad_up_bias: float32 [4096], P('mp')
- grad_down_weight: float32 [4096, 1024], P('mp')
- grad_down_bias: float32 [1024], replicated
- grad_dec_weight: float32 [1024, 512], replicated
- grad_dec_bias: float32 [512], replicated
- grad_mask_token: float32 [512], replicated
Inputs may be any that keep to these rules, and one draw needn't show every extreme that they name: `scene_ids`: within each group of 1024 rows (one dp index) scene ids start at 0 and rise by one at each scene boundary, never falling; scene 0 holds 256 to 512 rows, every other scene at least one. `owner_ids`: among the 256 rows of one device no owner is named more than 64 times; in each mp column one owner is named exactly 64 times by the rows of every device. `fill_slot`: in grid block e, slot s * 64 + r is named by exactly one cell when device (s, e % 4) has an r-th row (in row order) with owner e // 4, and by no cell otherwise. `patches`: magnitudes stay below 200.
All inputs are finite; a program needn't handle non-finite values.
Results may differ from a plain program's by a relative error of at most 0.013.
The roundings to bfloat16 on the way count: a program that leaves them out, or rounds other values in their place, can miss the bound.
Values may be sent and summed in bfloat16 or wider, within the bound.
A program may use at most 128 MiB of HBM per device.

v0:
```python
import jax
import jax.numpy as jnp
from jax import lax
from jax.sharding import PartitionSpec as P

HEAD_DIM = 64
QBLOCK = 512
NEG_FILL = -1000000000.0


def layer_norm(hidden, gain, bias_vec):
    centered = hidden - jnp.mean(hidden, axis=-1, keepdims=True)
    spread = jnp.mean(centered * centered, axis=-1, keepdims=True)
    return centered * lax.rsqrt(spread + 1e-06) * gain + bias_vec


def gelu_exact(values):
    return jax.nn.gelu(values, approximate=False)


def gather_rows(weight, data_par, model_par):
    rows, width = weight.shape
    part = rows // data_par
    mine = lax.dynamic_slice_in_dim(weight, lax.axis_index("dp") * part, part, 0)
    column = lax.all_gather(mine, "mp", axis=0)
    whole = lax.all_gather(column, "dp", axis=0)
    return whole.transpose(1, 0, 2, 3).reshape(model_par * rows, width)


def low(values):
    return values.astype(jnp.bfloat16)


def per_device(
    patches,
    scene_ids,
    owner_ids,
    fill_slot,
    norm1_gain,
    norm1_bias,
    qkv_weight,
    qv_bias,
    out_weight,
    out_bias,
    norm2_gain,
    norm2_bias,
    up_weight,
    up_bias,
    down_weight,
    down_bias,
    dec_weight,
    dec_bias,
    mask_token,
    positions,
    cotangent,
):
    row_count = patches.shape[0]
    model_par = lax.axis_size("mp")
    data_par = lax.axis_size("dp")
    group_rows = row_count * model_par
    total_rows = float(row_count * model_par * data_par)
    local_width = qkv_weight.shape[2]
    local_heads = local_width // HEAD_DIM
    score_scale = HEAD_DIM ** (-0.5)
    block_rows = min(QBLOCK, group_rows)
    block_starts = jnp.arange(group_rows // block_rows, dtype=jnp.int32) * block_rows
    capacity = 2 * row_count // data_par
    slot_count = capacity * data_par
    dec_width = dec_weight.shape[1]
    out_full = gather_rows(out_weight, data_par, model_par)
    inputs_f = patches.astype(jnp.float32)
    band_sums = lax.psum(
        (jnp.sum(inputs_f, axis=0), jnp.sum(inputs_f * inputs_f, axis=0)), ("dp", "mp")
    )
    band_mean = band_sums[0] / total_rows
    band_var = band_sums[1] / total_rows - band_mean * band_mean
    band_scale = lax.rsqrt(band_var + 1e-05)
    band_hat = (inputs_f - band_mean) * band_scale
    normed1 = layer_norm(band_hat, norm1_gain, norm1_bias).astype(jnp.bfloat16)
    norm1_all, scene_all = (
        lax.all_gather(normed1, "mp", axis=0, tiled=True),
        lax.all_gather(scene_ids, "mp", axis=0, tiled=True),
    )
    bias_three = jnp.stack([qv_bias[0], jnp.zeros_like(qv_bias[0]), qv_bias[1]])
    triples = (
        jnp.einsum("td,dcj->tcj", norm1_all, qkv_weight, preferred_element_type=jnp.float32)
        + bias_three
    ).astype(jnp.bfloat16)
    query_all = triples[:, 0].reshape(group_rows, local_heads, HEAD_DIM)
    key_all = triples[:, 1].reshape(group_rows, local_heads, HEAD_DIM)
    value_all = triples[:, 2].reshape(group_rows, local_heads, HEAD_DIM)

    def block_scores(first_row):
        query_blk = lax.dynamic_slice_in_dim(query_all, first_row, block_rows, 0)
        scene_blk = lax.dynamic_slice_in_dim(scene_all, first_row, block_rows, 0)
        scores = (
            jnp.einsum("qhd,khd->hqk", query_blk, key_all, preferred_element_type=jnp.float32)
            * score_scale
        )
        same_scene = (scene_blk[:, None] == scene_all[None, :])[None]
        return (jnp.where(same_scene, scores, NEG_FILL), query_blk)

    def attend_block(first_row):
        scores, query_blk = block_scores(first_row)
        row_max = jnp.max(scores, axis=-1, keepdims=True)
        exp_scores = jnp.exp(scores - row_max)
        row_total = jnp.sum(exp_scores, axis=-1, keepdims=True)
        softmax_w = (exp_scores / row_total).astype(jnp.bfloat16)
        mixed_rows = jnp.einsum(
            "hqk,khd->qhd", softmax_w, value_all, preferred_element_type=jnp.float32
        )
        return (mixed_rows.astype(jnp.bfloat16), (row_max + jnp.log(row_total))[..., 0])

    head_blocks, lse_blocks = lax.map(attend_block, block_starts)
    heads_out = head_blocks.reshape(group_rows, local_width)
    heads_rows = lax.all_to_all(heads_out, "mp", split_axis=0, concat_axis=1, tiled=True)
    attn_local = jnp.dot(heads_rows, out_full, preferred_element_type=jnp.float32)
    after_attn = band_hat + attn_local + out_bias
    normed2 = layer_norm(after_attn, norm2_gain, norm2_bias).astype(jnp.bfloat16)
    norm2_all = lax.all_gather(normed2, "mp", axis=0, tiled=True)
    pre_act = jnp.dot(norm2_all, up_weight, preferred_element_type=jnp.float32) + up_bias.astype(
        jnp.float32
    )
    act_rows = gelu_exact(pre_act).astype(jnp.bfloat16)
    mlp_part = low(jnp.dot(act_rows, down_weight, preferred_element_type=jnp.float32))
    proj_part = jnp.dot(mlp_part, dec_weight, preferred_element_type=jnp.float32)
    proj_sum = lax.psum_scatter(low(proj_part), "mp", scatter_dimension=0, tiled=True)
    direct = after_attn + down_bias
    projected = low(
        jnp.dot(low(direct), dec_weight, preferred_element_type=jnp.float32)
        + proj_sum.astype(jnp.float32)
        + dec_bias
    )
    owner_onehot = (owner_ids[:, None] == jnp.arange(data_par, dtype=jnp.int32)[None, :]).astype(
        jnp.int32
    )
    earlier = jnp.sum((jnp.cumsum(owner_onehot, axis=0) - owner_onehot) * owner_onehot, axis=1)
    send_slot = owner_ids * capacity + earlier
    slot_range = jnp.arange(slot_count, dtype=jnp.int32)
    send_onehot = (send_slot[:, None] == slot_range[None, :]).astype(jnp.bfloat16)
    outgoing = jnp.einsum(
        "rs,rc->sc", send_onehot, projected, preferred_element_type=jnp.float32
    ).astype(jnp.bfloat16)
    fill_onehot = (fill_slot[:, None] == slot_range[None, :]).astype(jnp.bfloat16)
    returning = jnp.einsum(
        "gs,gc->sc", fill_onehot, cotangent, preferred_element_type=jnp.float32
    ).astype(jnp.bfloat16)
    arrived, grad_back = (
        lax.all_to_all(
            outgoing.reshape(data_par, capacity, dec_width),
            "dp",
            split_axis=0,
            concat_axis=0,
            tiled=True,
        ),
        lax.all_to_all(
            returning.reshape(data_par, capacity, dec_width),
            "dp",
            split_axis=0,
            concat_axis=0,
            tiled=True,
        ),
    )
    placed = jnp.dot(
        fill_onehot, arrived.reshape(slot_count, dec_width), preferred_element_type=jnp.float32
    )
    masked = (fill_slot < 0)[:, None]
    decoder_in = (jnp.where(masked, mask_token, placed) + positions.astype(jnp.float32)).astype(
        jnp.bfloat16
    )
    grad_mask_local = jnp.sum(jnp.where(masked, cotangent.astype(jnp.float32), 0.0), axis=0)
    grad_proj = jnp.einsum(
        "rs,sc->rc",
        send_onehot,
        grad_back.reshape(slot_count, dec_width),
        preferred_element_type=jnp.float32,
    )
    grad_proj_low = grad_proj.astype(jnp.bfloat16)
    proj_grad_all = lax.all_gather(grad_proj_low, "mp", axis=0, tiled=True)
    grad_dec_local = jnp.einsum(
        "rd,rc->dc", low(direct), grad_proj_low, preferred_element_type=jnp.float32
    ) + jnp.einsum("rd,rc->dc", mlp_part, proj_grad_all, preferred_element_type=jnp.float32)
    grad_dec_bias_local = jnp.sum(grad_proj, axis=0)
    grad_block = jnp.einsum(
        "rc,dc->rd", grad_proj_low, dec_weight, preferred_element_type=jnp.float32
    )
    grad_down_bias_local = jnp.sum(low(grad_block).astype(jnp.float32), axis=0)
    grad_mlp_all = low(
        jnp.einsum("rc,dc->rd", proj_grad_all, dec_weight, preferred_element_type=jnp.float32)
    )
    grad_act = jnp.einsum(
        "tc,fc->tf", grad_mlp_all, down_weight, preferred_element_type=jnp.float32
    )
    grad_down_local = jnp.einsum(
        "tf,tc->fc", act_rows, grad_mlp_all, preferred_element_type=jnp.float32
    )
    down_sum = lax.psum(low(grad_down_local), "dp").astype(jnp.float32)
    gelu_val, gelu_back = jax.vjp(gelu_exact, pre_act)
    grad_pre = gelu_back(grad_act)[0].astype(jnp.bfloat16)
    grad_up_local = jnp.einsum("td,tf->df", norm2_all, grad_pre, preferred_element_type=jnp.float32)
    grad_up_bias_local = jnp.sum(grad_pre.astype(jnp.float32), axis=0)
    grad_norm2 = lax.psum_scatter(
        low(jnp.einsum("tf,df->td", grad_pre, up_weight, preferred_element_type=jnp.float32)),
        "mp",
        scatter_dimension=0,
        tiled=True,
    ).astype(jnp.float32)
    up_sum = lax.psum(low(grad_up_local), "dp").astype(jnp.float32)
    norm2_val, norm2_back = jax.vjp(layer_norm, after_attn, norm2_gain, norm2_bias)
    from_norm2, grad_gain2_local, grad_bias2_local = norm2_back(grad_norm2)
    grad_after = grad_block + from_norm2
    grad_attn = grad_after.astype(jnp.bfloat16)
    grad_out_bias_local = jnp.sum(grad_attn.astype(jnp.float32), axis=0)
    grad_out_rows = low(
        jnp.einsum("tj,tc->jc", heads_rows, grad_attn, preferred_element_type=jnp.float32)
    ).reshape(model_par, local_width, -1)
    out_part = lax.psum_scatter(grad_out_rows, "dp", scatter_dimension=1, tiled=True)
    out_part = lax.psum_scatter(out_part, "mp", scatter_dimension=0, tiled=True)
    out_sum = lax.all_gather(out_part[0], "dp", axis=0, tiled=True).astype(jnp.float32)
    grad_heads = lax.all_to_all(
        low(jnp.einsum("tc,jc->tj", grad_attn, out_full, preferred_element_type=jnp.float32)),
        "mp",
        split_axis=1,
        concat_axis=0,
        tiled=True,
    )
    grad_heads3 = grad_heads.reshape(group_rows, local_heads, HEAD_DIM)

    def back_block(carried, inputs):
        key_acc, value_acc = carried
        first_row, log_total = inputs
        scores, query_blk = block_scores(first_row)
        softmax_w = jnp.exp(scores - log_total[..., None])
        upstream = lax.dynamic_slice_in_dim(grad_heads3, first_row, block_rows, 0)
        value_acc = value_acc + jnp.einsum(
            "hqk,qhd->khd",
            softmax_w.astype(jnp.bfloat16),
            upstream,
            preferred_element_type=jnp.float32,
        )
        grad_probs = jnp.einsum(
            "qhd,khd->hqk", upstream, value_all, preferred_element_type=jnp.float32
        )
        inner_sum = jnp.sum(softmax_w * grad_probs, axis=-1, keepdims=True)
        grad_scores = (softmax_w * (grad_probs - inner_sum)).astype(jnp.bfloat16)
        grad_query = (
            jnp.einsum("hqk,khd->qhd", grad_scores, key_all, preferred_element_type=jnp.float32)
            * score_scale
        )
        key_acc = (
            key_acc
            + jnp.einsum("hqk,qhd->khd", grad_scores, query_blk, preferred_element_type=jnp.float32)
            * score_scale
        )
        return ((key_acc, value_acc), grad_query.astype(jnp.bfloat16))

    zero_heads = jnp.zeros((group_rows, local_heads, HEAD_DIM), jnp.float32)
    (key_grad, value_grad), query_blocks = lax.scan(
        back_block, (zero_heads, zero_heads), (block_starts, lse_blocks)
    )
    grad_triples = jnp.stack(
        [
            query_blocks.reshape(group_rows, local_width),
            key_grad.reshape(group_rows, local_width).astype(jnp.bfloat16),
            value_grad.reshape(group_rows, local_width).astype(jnp.bfloat16),
        ],
        axis=1,
    )
    grad_qkv_local = jnp.einsum(
        "td,tcj->dcj", norm1_all, grad_triples, preferred_element_type=jnp.float32
    )
    triple_sums = jnp.sum(grad_triples.astype(jnp.float32), axis=0)
    grad_qv_local = jnp.stack([triple_sums[0], triple_sums[2]])
    grad_norm1 = lax.psum_scatter(
        low(
            jnp.einsum("tcj,dcj->td", grad_triples, qkv_weight, preferred_element_type=jnp.float32)
        ),
        "mp",
        scatter_dimension=0,
        tiled=True,
    ).astype(jnp.float32)
    qkv_sum = lax.psum(low(grad_qkv_local), "dp").astype(jnp.float32)
    norm1_val, norm1_back = jax.vjp(layer_norm, band_hat, norm1_gain, norm1_bias)
    from_norm1, grad_gain1_local, grad_bias1_local = norm1_back(grad_norm1)
    grad_hat = grad_after + from_norm1
    dec_sum = lax.psum(low(grad_dec_local), ("dp", "mp")).astype(jnp.float32)
    summed_small = lax.psum((grad_qv_local, grad_up_bias_local), "dp")
    shared = lax.psum(
        (
            jnp.sum(grad_hat, axis=0),
            jnp.sum(grad_hat * band_hat, axis=0),
            grad_gain1_local,
            grad_bias1_local,
            grad_gain2_local,
            grad_bias2_local,
            grad_out_bias_local,
            grad_down_bias_local,
            grad_dec_bias_local,
            grad_mask_local,
        ),
        ("dp", "mp"),
    )
    grad_patches = band_scale * (
        grad_hat - shared[0] / total_rows - band_hat * (shared[1] / total_rows)
    )
    return (
        decoder_in,
        grad_patches,
        shared[2],
        shared[3],
        qkv_sum,
        summed_small[0],
        out_sum,
        shared[6],
        shared[4],
        shared[5],
        up_sum,
        summed_small[1],
        down_sum,
        shared[7],
        dec_sum,
        shared[8],
        shared[9],
    )


def solution(mesh):
    in_specs = (
        P(("dp", "mp"), None),
        P(("dp", "mp")),
        P(("dp", "mp")),
        P(("dp", "mp")),
        P(),
        P(),
        P(None, None, "mp"),
        P(None, "mp"),
        P("mp", None),
        P(),
        P(),
        P(),
        P(None, "mp"),
        P("mp"),
        P("mp", None),
        P(),
        P(),
        P(),
        P(),
        P(("dp", "mp"), None),
        P(("dp", "mp"), None),
    )
    out_specs = (
        P(("dp", "mp"), None),
        P(("dp", "mp"), None),
        P(),
        P(),
        P(None, None, "mp"),
        P(None, "mp"),
        P("mp", None),
        P(),
        P(),
        P(),
        P(None, "mp"),
        P("mp"),
        P("mp", None),
        P(),
        P(),
        P(),
        P(),
    )
    return jax.shard_map(
        per_device, mesh=mesh, in_specs=in_specs, out_specs=out_specs, check_vma=False
    )
```

profile of v0, /device:TPU:0, one launch (start us, length us, event | category | flops | bytes accessed | tf_op | source)
XLA Modules:
  0.0 733.2 jit_solution(15494136100213632518)
XLA Ops:
  8.6 42.1 %all-reduce.1 = (f32[1024]{0:T(1024)S(1)}, f32[1024]{0:T(1024)S(1)}) all-reduce(f32[1024]{0:T(1024)S(1)} %get-tuple-element.181, f32[1024]{0:T(1024)S(1)} %get-tuple-element.180), channel_id=1, replica_groups=mesh['dp'=8,'mp'=4] {'dp','mp'}, use_global_device_ids=true, to_apply=%region_6.7 | all-reduce | flops 2048 | bytes 16384 | tf_op jit(solution)/shard_map/psum | solution.py:72
  55.6 3.0 fusion.56
  58.6 4.1 all-to-all-start.2
  63.7 17.0 %all-gather = bf16[128,1024]{1,0:T(8,128)(2,1)} all-gather(bf16[32,1024]{1,0:T(8,128)(2,1)S(1)} %constant_dynamic-slice_fusion), channel_id=2, replica_groups=mesh['dp'=8,'mp'=4] {'mp'}, dimensions={0}, use_global_device_ids=true | all-gather | bytes 327680 | tf_op jit(solution)/shard_map/all_gather | solution.py:25
  80.8 10.5 %all-gather.3 = s32[4,1,256]{2,1,0:T(1,128)S(1)} all-gather(s32[1,1,256]{2,1,0:T(1,128)S(1)} %bitcast.166), channel_id=1, replica_groups=mesh['dp'=8,'mp'=4] {'mp'}, dimensions={0}, use_global_device_ids=true | all-gather | bytes 5120 | tf_op jit(solution)/shard_map/all_gather | solution.py:82
  92.4 13.1 %all-gather.9.cloned.1.call-done = bf16[1024,1024]{1,0:T(8,128)(2,1)} async-done(((bf16[256,1024]{1,0:T(8,128)(2,1)}), bf16[1024,1024]{1,0:T(8,128)(2,1)}) %all-gather.9.cloned.1.call-update) | async-done | bytes 2097168 | tf_op jit(solution)/shard_map/all_gather | solution.py:81
  105.5 3.9 add_convert_fusion.1
  111.2 22.3 %while.27 = (s32[]{:T(128)}, bf16[2,512,4,64]{1,3,2,0:T(8,128)(2,1)}, f32[2,4,512]{2,1,0:T(4,128)S(1)}, s32[2]{0:T(128)S(1)}, s32[1024]{0:T(1024)S(1)}, /*index=...) while((s32[]{:T(128)}, ...), condition=%wide.region_12.13_spmd, body=%wide.region_9.12_spmd.sunk | while | flops 562690048 | bytes 35203332 | solution.py:114
  118.5 3.0 fusion.170
  129.7 3.0 fusion.170
  136.7 2.9 all_to_all.32
  141.5 4.1 all-to-all-start
  145.9 2.7 fusion.102
  148.7 3.2 copy.77
  151.9 8.4 %all-to-all-done = bf16[4,256,256]{1,2,0:T(8,128)(2,1)} async-done(((bf16[4,256,256]{1,2,0:T(8,128)(2,1)}), bf16[4,256,256]{1,2,0:T(8,128)(2,1)}, u32[]{:S(2)}, u32[]{:S(2)}) %all-to-all-start) | async-done | bytes 524320 | tf_op jit(solution)/shard_map/all_to_all | solution.py:116
  165.1 13.0 %all-gather.13.cloned.1.call-done = bf16[1024,512]{1,0:T(8,128)(2,1)} async-done(((bf16[256,512]{1,0:T(8,128)(2,1)}), bf16[1024,512]{1,0:T(8,128)(2,1)}) %all-gather.13.cloned.1.call-update) | async-done | bytes 1048592 | tf_op jit(solution)/shard_map/all_gather | solution.py:179
  178.1 4.1 convolution_convert_fusion.4
  182.2 42.9 %all-gather.11.cloned.1.call-done = bf16[1024,1024]{1,0:T(8,128)(2,1)} async-done(((bf16[256,1024]{1,0:T(8,128)(2,1)}), bf16[1024,1024]{1,0:T(8,128)(2,1)}) %all-gather.11.cloned.1.call-update) | async-done | bytes 2097168 | tf_op jit(solution)/shard_map/all_gather | solution.py:120
  225.1 4.7 fusion.106
  229.9 13.9 %convert_reduce_fusion = (f32[1024]{0:T(1024)}, bf16[1024,1024]{1,0:T(8,128)(2,1)S(1)}, f32[1024,1024]{1,0:T(8,128)}) fusion(f32[1024,1024]{1,0:T(8,128)S(1)} %fusion.106, f32[1024]{0:T(1024)S(1)} %convert_element_type.184, bf16[1024,1024]{1,0:T(8,128)(2,1)S(1)} %copy-done.61, bf16[1024,1024]{1,0:T(8,128)(2,1)S(1)} %copy-done), kind=kOutput, calls=%fused_computation.48 | convolution fusion | flops 2226125824 | bytes 14688256 | tf_op jit(solution)/shard_map/tc,fc->tf/dot_general | solution.py:191
  245.2 3.7 convolution_convert_fusion.3
  248.9 42.5 %reduce-scatter.8.cloned.1.call-done = bf16[256,1024]{1,0:T(8,128)(2,1)} async-done(((bf16[1024,1024]{1,0:T(8,128)(2,1)}), bf16[256,1024]{1,0:T(8,128)(2,1)}) %reduce-scatter.8.cloned.1.call-update) | async-done | bytes 524304 | tf_op jit(solution)/shard_map/reduce_scatter | solution.py:202
  298.8 3.1 convolution_convert_fusion.2
  302.1 4.6 multiply_convert_fusion.1
  312.7 4.4 fusion.107
  317.2 3.8 convolution_convert_fusion
  322.5 3.5 all-to-all-start.3
  326.0 3.1 add_convert_fusion.2
  329.2 6.1 convolution_convert_fusion.1
  335.3 5.1 all-to-all-done.3
  343.7 30.6 %while.28 = (s32[]{:T(128)}, f32[1024,4,64]{0,2,1:T(8,128)S(1)}, f32[1024,4,64]{0,2,1:T(8,128)}, bf16[2,512,4,64]{1,3,2,0:T(8,128)(2,1)}, s32[2]{0:T(128)S(1)}, ...) while((s32[]{:T(128)}, f32[1024,4,64]{0,2,1:T(8,128)S(1)}, ...), condition=%wide.region_21.22_spmd.clone, body=%wide.region_19.21_spmd.clone.sunk | while | flops 1375729664 | bytes 84740432 | solution.py:258
  351.0 3.3 multiply_reduce_fusion.3
  366.2 3.3 multiply_reduce_fusion.3
  378.6 4.6 fusion.50
  383.9 4.6 bitcast_convert_fusion
  388.6 2.8 convolution_convert_fusion.8
  391.4 3.7 all-to-all-start.1
  396.6 110.9 %all-reduce.7.cloned.1.call-done = bf16[1024,512]{1,0:T(8,128)(2,1)} async-done(((bf16[1024,512]{1,0:T(8,128)(2,1)}), bf16[1024,512]{1,0:T(8,128)(2,1)}) %all-reduce.7.cloned.1.call-update) | async-done | bytes 1048592 | tf_op jit(solution)/shard_map/psum | solution.py:286
  507.5 2.8 convert_element_type.221
  510.4 3.1 add_convert_fusion.3
  513.7 13.4 %all-reduce.2 = (f32[2,256]{1,0:T(2,128)}, f32[1024]{0:T(1024)}) all-reduce(f32[2,256]{1,0:T(2,128)S(1)} %pad_maximum_fusion.2, f32[1024]{0:T(1024)S(1)} %copy-done.49), channel_id=1, replica_groups=mesh['dp'=8,'mp'=4] {'dp'}, use_global_device_ids=true, to_apply=%region_35.36 | all-reduce | flops 1536 | bytes 12288 | tf_op jit(solution)/shard_map/psum | solution.py:287
  527.1 82.7 %all-reduce.9.cloned.1.call-done = (bf16[1024,3,256]{2,0,1:T(8,128)(2,1)}, bf16[1024,1024]{1,0:T(8,128)(2,1)}, bf16[1024,1024]{1,0:T(8,128)(2,1)}) async-done(((bf16[1024,3,256]{2,0,1:T(8,128)(2,1)}, bf16[1024,1024]{1,0:T(8,128)(2,1)}, bf16[1024,1024]{1,0:T(8,128)(2,1)}), (bf16[1024,3,256]{2,0,1:T(8,128)(2,1)}, bf16[1024,1024]{1,0:T(8,128)(2,1)}, bf16[1024,1024]{1,0:T(8,128)(2,1)})) %all-reduce.9.cloned.1.call-update) | async-done | bytes 5767184 | tf_op jit(solution)/shard_map/psum | solution.py:282
  609.9 3.5 convert_element_type.208
  618.4 13.7 %reduce-scatter.14.cloned.1.call-done = bf16[1,32,1024]{2,1,0:T(8,128)(2,1)} async-done(((bf16[4,32,1024]{2,1,0:T(8,128)(2,1)}), bf16[1,32,1024]{2,1,0:T(8,128)(2,1)}) %reduce-scatter.14.cloned.1.call-update) | async-done | bytes 65552 | tf_op jit(solution)/shard_map/reduce_scatter | solution.py:218
  632.1 10.1 %all-gather.2 = bf16[1,256,1024]{2,1,0:T(8,128)(2,1)S(1)} all-gather(bf16[1,32,1024]{2,1,0:T(8,128)(2,1)} %reduce-scatter.14.cloned.1.call-done), channel_id=4, replica_groups=mesh['dp'=8,'mp'=4] {'dp'}, dimensions={1}, use_global_device_ids=true | all-gather | bytes 589824 | tf_op jit(solution)/shard_map/all_gather | solution.py:219
  643.2 33.0 %reduce-scatter.10.cloned.1.call-done = bf16[256,1024]{1,0:T(8,128)(2,1)} async-done(((bf16[1024,1024]{1,0:T(8,128)(2,1)}), bf16[256,1024]{1,0:T(8,128)(2,1)}) %reduce-scatter.10.cloned.1.call-update) | async-done | bytes 524304 | tf_op jit(solution)/shard_map/reduce_scatter | solution.py:274
  679.7 3.6 fusion.97
  683.4 40.7 %all-reduce = (f32[1024]{0:T(1024)S(1)}, f32[1024]{0:T(1024)S(1)}, f32[1024]{0:T(1024)}, f32[1024]{0:T(1024)}, f32[1024]{0:T(1024)}, /*index=5*/f32[1024]{0:T(10...) all-reduce(f32[1024]{0:T(1024)S(1)} %get-tuple-element.176, ...), channel_id=1, replica_groups=mesh['dp'=8,'mp'=4] {'dp','mp'}, use_global_device_ids=true, to_apply=%region_28.29 | all-reduce | flops 9216 | bytes 73728 | tf_op jit(solution)/shard_map/psum | solution.py:288
  (263 shorter events, 90.6 us)
Async XLA Ops:
  7.2 222.6 %copy-start = (bf16[1024,1024]{1,0:T(8,128)(2,1)S(1)}, bf16[1024,1024]{1,0:T(8,128)(2,1)}, u32[]{:S(2)}) copy-start(bf16[1024,1024]{1,0:T(8,128)(2,1)} %param.39) | copy-start | bytes 6291460
  7.2 73.6 %copy-start.52 = (f32[2,256]{1,0:T(2,128)S(1)}, f32[2,256]{1,0:T(2,128)}, u32[]{:S(2)}) copy-start(f32[2,256]{1,0:T(2,128)} %param.32) | copy-start | bytes 6148
  7.2 73.6 %copy-start.53 = (s32[256]{0:T(256)S(1)}, s32[256]{0:T(256)}, u32[]{:S(2)}) copy-start(s32[256]{0:T(256)} %param.26) | copy-start | bytes 3076
  7.2 84.1 %copy-start.43 = (s32[256]{0:T(256)S(1)}, s32[256]{0:T(256)}, u32[]{:S(2)}) copy-start(s32[256]{0:T(256)} %param.27) | copy-start | bytes 3076
  7.2 98.2 %all-gather.9.cloned.1.call-start = ((), (), s32[]{:S(2)}) async-start(), calls=%async_computation.9 | async-start | bytes 2621440 | tf_op jit(solution)/shard_map/all_gather | solution.py:81
  50.7 109.6 %copy-start.27 = (f32[1024]{0:T(1024)}, f32[1024]{0:T(1024)S(1)}, u32[]{:S(2)}) copy-start(f32[1024]{0:T(1024)S(1)} %get-tuple-element.257) | copy-start | bytes 12292
  50.7 109.6 %copy-start.29 = (f32[1024]{0:T(1024)}, f32[1024]{0:T(1024)S(1)}, u32[]{:S(2)}) copy-start(f32[1024]{0:T(1024)S(1)} %get-tuple-element.258) | copy-start | bytes 12292
  52.0 10.8 %copy-start.33 = (f32[256]{0:T(256)}, f32[256]{0:T(256)S(1)}, u32[]{:S(2)}) copy-start(f32[256]{0:T(256)S(1)} %broadcast_multiply_fusion.4) | copy-start | bytes 3076
  53.4 9.4 %copy-start.41 = (f32[256]{0:T(256)}, f32[256]{0:T(256)S(1)}, u32[]{:S(2)}) copy-start(f32[256]{0:T(256)S(1)} %fusion.76) | copy-start | bytes 3076
  58.6 82.9 %all-to-all-start.2 = ((bf16[8,64,512]{2,1,0:T(8,128)(2,1)}), bf16[8,64,512]{2,1,0:T(8,128)(2,1)}, u32[]{:S(2)}, u32[]{:S(2)}) async-start(bf16[8,64,512]{2,1,0:T(8,128)(2,1)} %bitcast.21), calls=%async_computation.3 | async-start | bytes 1048576 | tf_op jit(solution)/shard_map/all_to_all | solution.py:156
  62.8 85.9 %all-gather.15.cloned.1.call-start = ((), (), s32[]{:S(2)}) async-start(), calls=%async_computation.18 | async-start | bytes 2359296 | tf_op jit(solution)/shard_map/all_gather | solution.py:26
  136.7 23.6 %copy-start.2 = (bf16[256,1024]{1,0:T(8,128)(2,1)S(1)}, bf16[256,1024]{1,0:T(8,128)(2,1)}, u32[]{:S(2)}) copy-start(bf16[256,1024]{1,0:T(8,128)(2,1)} %param.25) | copy-start | bytes 1572868
  136.7 23.6 %copy-start.35 = (f32[1024]{0:T(1024)S(1)}, f32[1024]{0:T(1024)}, u32[]{:S(2)}) copy-start(f32[1024]{0:T(1024)} %param.34) | copy-start | bytes 12292
  141.5 18.8 %all-to-all-start = ((bf16[4,256,256]{1,2,0:T(8,128)(2,1)}), bf16[4,256,256]{1,2,0:T(8,128)(2,1)}, u32[]{:S(2)}, u32[]{:S(2)}) async-start(bf16[4,256,256]{1,2,0:T(8,128)(2,1)} %copy.76), calls=%async_computation | async-start | bytes 1048576 | tf_op jit(solution)/shard_map/all_to_all | solution.py:116
  145.7 32.4 %all-gather.13.cloned.1.call-start = ((), (), s32[]{:S(2)}) async-start(), calls=%async_computation.12 | async-start | bytes 1310720 | tf_op jit(solution)/shard_map/all_gather | solution.py:179
  148.6 76.5 %all-gather.11.cloned.1.call-start = ((), (), s32[]{:S(2)}) async-start(), calls=%async_computation.10 | async-start | bytes 2621440 | tf_op jit(solution)/shard_map/all_gather | solution.py:120
  148.7 15.2 %copy-start.32 = (f32[1024]{0:T(1024)S(1)}, f32[1024]{0:T(1024)}, u32[]{:S(2)}) copy-start(f32[1024]{0:T(1024)} %param.35) | copy-start | bytes 12292
  148.7 15.2 %copy-start.46 = (f32[1024]{0:T(1024)S(1)}, f32[1024]{0:T(1024)}, u32[]{:S(2)}) copy-start(f32[1024]{0:T(1024)} %param.36) | copy-start | bytes 12292
  151.9 13.1 %copy-start.50 = (bf16[1024]{0:T(1024)(128)(2,1)S(1)}, bf16[1024]{0:T(1024)(128)(2,1)}, u32[]{:S(2)}) copy-start(bf16[1024]{0:T(1024)(128)(2,1)} %param.38) | copy-start | bytes 6148
  165.0 126.5 %reduce-scatter.8.cloned.1.call-start = ((), (), s32[]{:S(2)}) async-start(), calls=%async_computation.13 | async-start | bytes 2621440 | tf_op jit(solution)/shard_map/reduce_scatter | solution.py:202
  229.8 14.0 %copy-start.13 = (f32[1024,1024]{1,0:T(8,128)}, f32[1024,1024]{1,0:T(8,128)S(1)}, u32[]{:S(2)}) copy-start(f32[1024,1024]{1,0:T(8,128)S(1)} %fusion.106) | copy-start | bytes 12582916
  229.9 15.3 %copy-start.56 = (bf16[1024,1024]{1,0:T(8,128)(2,1)S(1)}, bf16[1024,1024]{1,0:T(8,128)(2,1)}, u32[]{:S(2)}) copy-start(bf16[1024,1024]{1,0:T(8,128)(2,1)} %param.37) | copy-start | bytes 6291460
  248.8 47.9 %copy-start.14 = (bf16[256,512]{1,0:T(8,128)(2,1)S(1)}, bf16[256,512]{1,0:T(8,128)(2,1)}, u32[]{:S(2)}) copy-start(bf16[256,512]{1,0:T(8,128)(2,1)} %get-tuple-element.254) | copy-start | bytes 786436
  248.9 134.4 %reduce-scatter.12.cloned.1.call-start = ((), (), s32[]{:S(2)}) async-start(), calls=%async_computation.15 | async-start | bytes 2359296 | tf_op jit(solution)/shard_map/reduce_scatter | solution.py:217
  301.9 86.7 %reduce-scatter.6.cloned.1.call-start = ((), (), s32[]{:S(2)}) async-start(), calls=%async_computation.11 | async-start | bytes 1310720 | tf_op jit(solution)/shard_map/reduce_scatter | solution.py:127
  322.5 17.9 %all-to-all-start.3 = ((bf16[256,4,256]{2,0,1:T(8,128)(2,1)}), bf16[256,4,256]{2,0,1:T(8,128)(2,1)S(1)}, u32[]{:S(2)}, u32[]{:S(2)}) async-start(bf16[256,4,256]{2,0,1:T(8,128)(2,1)} %bitcast.160), calls=%async_computation.5 | async-start | bytes 1048576 | tf_op jit(solution)/shard_map/all_to_all | solution.py:220
  326.0 181.6 %all-reduce.7.cloned.1.call-start = ((), (), s32[]{:S(2)}) async-start(), calls=%async_computation.17 | async-start | bytes 2097152 | tf_op jit(solution)/shard_map/psum | solution.py:286
  329.1 14.5 %copy-start.5 = (bf16[1024,4,64]{0,2,1:T(8,128)(2,1)S(1)}, bf16[1024,4,64]{0,2,1:T(8,128)(2,1)}, u32[]{:S(2)}) copy-start(bf16[1024,4,64]{0,2,1:T(8,128)(2,1)} %copy-done.4) | copy-start | bytes 1572868
  329.1 14.5 %copy-start.10 = (bf16[1024,4,64]{0,2,1:T(8,128)(2,1)S(1)}, bf16[1024,4,64]{0,2,1:T(8,128)(2,1)}, u32[]{:S(2)}) copy-start(bf16[1024,4,64]{0,2,1:T(8,128)(2,1)} %get-tuple-element.484) | copy-start | bytes 1572868
  329.2 280.7 %all-reduce.9.cloned.1.call-start = ((), (), s32[]{:S(2)}) async-start(), calls=%async_computation.19 | async-start | bytes 11534336 | tf_op jit(solution)/shard_map/psum | solution.py:282
  383.2 248.9 %reduce-scatter.14.cloned.1.call-start = ((), (), s32[]{:S(2)}) async-start(), calls=%async_computation.16 | async-start | bytes 327680 | tf_op jit(solution)/shard_map/reduce_scatter | solution.py:218
  383.8 292.4 %reduce-scatter.10.cloned.1.call-start = ((), (), s32[]{:S(2)}) async-start(), calls=%async_computation.14 | async-start | bytes 2621440 | tf_op jit(solution)/shard_map/reduce_scatter | solution.py:274
  388.5 121.8 %copy-start.59 = (f32[512]{0:T(512)S(1)}, f32[512]{0:T(512)}, u32[]{:S(2)}) copy-start(f32[512]{0:T(512)} %param.43) | copy-start | bytes 6148
  391.4 119.0 %all-to-all-start.1 = ((bf16[8,64,512]{2,1,0:T(8,128)(2,1)}), bf16[8,64,512]{2,1,0:T(8,128)(2,1)S(1)}, u32[]{:S(2)}, u32[]{:S(2)}) async-start(bf16[8,64,512]{2,1,0:T(8,128)(2,1)} %bitcast.19), calls=%async_computation.2 | async-start | bytes 1048576 | tf_op jit(solution)/shard_map/all_to_all | solution.py:149
  396.6 117.2 %copy-start.49 = (f32[1024]{0:T(1024)S(1)}, f32[1024]{0:T(1024)}, u32[]{:S(2)}) copy-start(f32[1024]{0:T(1024)} %get-tuple-element.237) | copy-start | bytes 12292
  615.8 60.4 %copy-start.3 = (bf16[256,1024]{1,0:T(8,128)(2,1)S(1)}, bf16[256,1024]{1,0:T(8,128)(2,1)}, u32[]{:S(2)}) copy-start(bf16[256,1024]{1,0:T(8,128)(2,1)} %param.25) | copy-start | bytes 1572868
  615.8 60.4 %copy-start.28 = (f32[1024]{0:T(1024)S(1)}, f32[1024]{0:T(1024)}, u32[]{:S(2)}) copy-start(f32[1024]{0:T(1024)} %copy-done.27) | copy-start | bytes 12292
  615.8 60.4 %copy-start.30 = (f32[1024]{0:T(1024)S(1)}, f32[1024]{0:T(1024)}, u32[]{:S(2)}) copy-start(f32[1024]{0:T(1024)} %copy-done.29) | copy-start | bytes 12292
  615.8 60.4 %copy-start.31 = (f32[1024]{0:T(1024)S(1)}, f32[1024]{0:T(1024)}, u32[]{:S(2)}) copy-start(f32[1024]{0:T(1024)} %param.29) | copy-start | bytes 12292
  615.8 60.4 %copy-start.34 = (f32[256]{0:T(256)S(1)}, f32[256]{0:T(256)}, u32[]{:S(2)}) copy-start(f32[256]{0:T(256)} %copy-done.33) | copy-start | bytes 3076
  615.9 62.1 %copy-start.42 = (f32[256]{0:T(256)S(1)}, f32[256]{0:T(256)}, u32[]{:S(2)}) copy-start(f32[256]{0:T(256)} %copy-done.41) | copy-start | bytes 3076
  615.9 62.1 %copy-start.40 = (f32[256]{0:T(256)S(1)}, f32[256]{0:T(256)}, u32[]{:S(2)}) copy-start(f32[256]{0:T(256)} %copy-done.39) | copy-start | bytes 3076
  615.9 63.8 %copy-start.45 = (f32[256]{0:T(256)S(1)}, f32[256]{0:T(256)}, u32[]{:S(2)}) copy-start(f32[256]{0:T(256)} %copy-done.44) | copy-start | bytes 3076
  618.4 65.0 %copy-start.36 = (f32[1024]{0:T(1024)S(1)}, f32[1024]{0:T(1024)}, u32[]{:S(2)}) copy-start(f32[1024]{0:T(1024)} %get-tuple-element.171) | copy-start | bytes 12292
  618.4 65.0 %copy-start.37 = (f32[1024]{0:T(1024)S(1)}, f32[1024]{0:T(1024)}, u32[]{:S(2)}) copy-start(f32[1024]{0:T(1024)} %get-tuple-element.177) | copy-start | bytes 12292
  618.4 65.0 %copy-start.38 = (f32[1024]{0:T(1024)S(1)}, f32[1024]{0:T(1024)}, u32[]{:S(2)}) copy-start(f32[1024]{0:T(1024)} %get-tuple-element.240) | copy-start | bytes 12292
  618.4 65.0 %copy-start.51 = (f32[512]{0:T(512)S(1)}, f32[512]{0:T(512)}, u32[]{:S(2)}) copy-start(f32[512]{0:T(512)} %get-tuple-element.253) | copy-start | bytes 6148
  676.3 50.2 %copy-start.1 = (bf16[1024,1024]{1,0:T(8,128)(2,1)S(1)}, bf16[1024,1024]{1,0:T(8,128)(2,1)}, u32[]{:S(2)}) copy-start(bf16[1024,1024]{1,0:T(8,128)(2,1)} %param.39) | copy-start | bytes 6291460
  (38 other events, 116.2 us)
Sparse Core Ops, SparseCore 0:
  55.7 49.7 all-gather.8
  107.4 26.6 all-gather.14
  148.7 29.2 all-gather.12
  180.1 45.0 all-gather.10
  249.0 42.4 reduce-scatter.7
  302.0 40.2 reduce-scatter.11
  345.2 27.3 reduce-scatter.5
  378.3 129.2 all-reduce.6
  512.3 97.5 all-reduce.8
  612.0 20.0 reduce-scatter.13
  634.4 41.8 reduce-scatter.9
where the time goes:
time: 743 us; the launch traced here: 733 us
  waiting for transfers between devices  366 us (49%)
  blocking collectives  134 us (18%)
  matrix products  111 us (15%)
  other arithmetic  52.9 us (7%)
  local copies, waits for them, and re-layouts  30 us (4%)
  starting transfers between devices  16.3 us (2%)
  between operations  14.9 us (2%)
  loops' own time  8.35 us (1%)
    psum x1, waiting for transfers between devices, per_device(): dec_sum = lax.psum(low(grad_dec_local), ('dp', 'mp')).astype(jnp.float32)  111 us
    psum x1, waiting for transfers between devices, per_device(): qkv_sum = lax.psum(low(grad_qkv_local), 'dp').astype(jnp.float32)  82.7 us
    all_gather x1, waiting for transfers between devices, per_device(): norm2_all = lax.all_gather(normed2, 'mp', axis=0, tiled=True)  42.9 us
    reduce_scatter x1, waiting for transfers between devices, per_device(): lax.psum_scatter(low(jnp.einsum('tf,df->td', grad_pre, up_weight, preferr...  42.5 us
    psum x1, blocking collectives, per_device(): lax.psum((jnp.sum(inputs_f, axis=0), jnp.sum(inputs_f * inputs_f, axis=0)...  42.1 us
    psum x1, blocking collectives, per_device(): lax.psum((jnp.sum(grad_hat, axis=0), jnp.sum(grad_hat * band_hat, axis=0)...  40.7 us
    reduce_scatter x1, waiting for transfers between devices, per_device(): lax.psum_scatter(low(jnp.einsum('tcj,dcj->td', grad_triples, qkv_weight,...  33 us
    all_gather x1, blocking collectives, gather_rows(): column = lax.all_gather(mine, 'mp', axis=0)  17 us
  transfers between devices with their start and end apart: 15, of which 10 were waited for; matrix products, arithmetic and copies ran while one was open for 19% of the time, Pallas kernels for 0%

commit v1 on v0

--- a/solution.py
+++ b/solution.py
@@ -6,6 +6,29 @@
 HEAD_DIM = 64
 QBLOCK = 512
 NEG_FILL = -1000000000.0
+
+
+def in_order(pieces, dim):
+    pieces = jnp.moveaxis(pieces, 0, dim)
+    dims = pieces.shape
+    return pieces.reshape(*dims[:dim], dims[dim] * dims[dim + 1], *dims[dim + 2 :])
+
+
+def collected_by_bits(array, axis):
+    devices, index = (lax.axis_size(axis), lax.axis_index(axis))
+    pieces, bit = (array[None], 1)
+    while bit < devices:
+        received = lax.ppermute(pieces, axis, [(i, i ^ bit) for i in range(devices)])
+        low = index & bit == 0
+        pieces = jnp.concatenate(
+            [jnp.where(low, pieces, received), jnp.where(low, received, pieces)]
+        )
+        bit *= 2
+    return pieces
+
+
+def collect(value, axis, dim):
+    return in_order(collected_by_bits(value, axis), dim)
 
 
 def layer_norm(hidden, gain, bias_vec):
@@ -117,7 +140,7 @@
     attn_local = jnp.dot(heads_rows, out_full, preferred_element_type=jnp.float32)
     after_attn = band_hat + attn_local + out_bias
     normed2 = layer_norm(after_attn, norm2_gain, norm2_bias).astype(jnp.bfloat16)
-    norm2_all = lax.all_gather(normed2, "mp", axis=0, tiled=True)
+    norm2_all = collect(normed2, "mp", 0)
     pre_act = jnp.dot(norm2_all, up_weight, preferred_element_type=jnp.float32) + up_bias.astype(
         jnp.float32
     )

time: 743 us -> 762 us (1.026)
  waiting for transfers between devices: 366 us -> 384 us
    all_gather x1 -> x0, waiting for transfers between devices: 42.9 us -> none  [per_device(): norm2_all = lax.all_gather(normed2, 'mp', axis=0, tiled=True)]
    all_gather x1, waiting for transfers between devices: 13 us -> 44.5 us  [per_device(): proj_grad_all = lax.all_gather(grad_proj_low, 'mp', axis=0, tiled=True)]
    ppermute x0 -> x2, waiting for transfers between devices: none -> 19.1 us  [collected_by_bits(): lax.ppermute(pieces, axis, [(i, i ^ bit) for i in range(devices)])]
  transfers between devices with their start and end apart: 15 -> 16, of which waited for: 10 -> 12; matrix products, arithmetic and copies ran while one was open for 19% -> 18% of each run, Pallas kernels for 0% -> 0%
where the time goes in v1:
time: 762 us; the launch traced here: 752 us
  waiting for transfers between devices  384 us (50%)
  blocking collectives  133 us (17%)
  matrix products  107 us (14%)
  other arithmetic  56.5 us (7%)
  local copies, waits for them, and re-layouts  30.9 us (4%)
  starting transfers between devices  16.6 us (2%)
  between operations  15.2 us (2%)
  loops' own time  8.07 us (1%)
    psum x1, waiting for transfers between devices, per_device(): dec_sum = lax.psum(low(grad_dec_local), ('dp', 'mp')).astype(jnp.float32)  111 us
    psum x1, waiting for transfers between devices, per_device(): qkv_sum = lax.psum(low(grad_qkv_local), 'dp').astype(jnp.float32)  82.7 us
    all_gather x1, waiting for transfers between devices, per_device(): proj_grad_all = lax.all_gather(grad_proj_low, 'mp', axis=0, tiled=True)  44.5 us
    reduce_scatter x1, waiting for transfers between devices, per_device(): lax.psum_scatter(low(jnp.einsum('tf,df->td', grad_pre, up_weight, preferr...  42.6 us
    psum x1, blocking collectives, per_device(): lax.psum((jnp.sum(inputs_f, axis=0), jnp.sum(inputs_f * inputs_f, axis=0)...  42.1 us
    psum x1, blocking collectives, per_device(): lax.psum((jnp.sum(grad_hat, axis=0), jnp.sum(grad_hat * band_hat, axis=0)...  40.7 us
    reduce_scatter x1, waiting for transfers between devices, per_device(): lax.psum_scatter(low(jnp.einsum('tcj,dcj->td', grad_triples, qkv_weight,...  32.9 us
    ppermute x2, waiting for transfers between devices, collected_by_bits(): lax.ppermute(pieces, axis, [(i, i ^ bit) for i in range(devices)])  19.1 us
  transfers between devices with their start and end apart: 16, of which 12 were waited for; matrix products, arithmetic and copies ran while one was open for 18% of the time, Pallas kernels for 0%

profile of v1, /device:TPU:0, one launch (start us, length us, event | category | flops | bytes accessed | tf_op | source)
XLA Modules:
  0.0 751.7 jit_solution(10242478951210121632)
XLA Ops:
  8.6 42.1 %all-reduce.1 = (f32[1024]{0:T(1024)S(1)}, f32[1024]{0:T(1024)S(1)}) all-reduce(f32[1024]{0:T(1024)S(1)} %get-tuple-element.181, f32[1024]{0:T(1024)S(1)} %get-tuple-element.180), channel_id=1, replica_groups=mesh['dp'=8,'mp'=4] {'dp','mp'}, use_global_device_ids=true, to_apply=%region_6.7 | all-reduce | flops 2048 | bytes 16384 | tf_op jit(solution)/shard_map/psum | solution.py:95
  56.5 16.7 %all-gather = bf16[128,1024]{1,0:T(8,128)(2,1)} all-gather(bf16[32,1024]{1,0:T(8,128)(2,1)S(1)} %constant_dynamic-slice_fusion), channel_id=2, replica_groups=mesh['dp'=8,'mp'=4] {'mp'}, dimensions={0}, use_global_device_ids=true | all-gather | bytes 327680 | tf_op jit(solution)/shard_map/all_gather | solution.py:48
  74.0 10.0 %all-gather.3 = s32[4,1,256]{2,1,0:T(1,128)S(1)} all-gather(s32[1,1,256]{2,1,0:T(1,128)} %bitcast.174), channel_id=1, replica_groups=mesh['dp'=8,'mp'=4] {'mp'}, dimensions={0}, use_global_device_ids=true | all-gather | bytes 5120 | tf_op jit(solution)/shard_map/all_gather | solution.py:105
  84.2 18.6 %all-gather.8.cloned.1.call-done = bf16[1024,1024]{1,0:T(8,128)(2,1)} async-done(((bf16[256,1024]{1,0:T(8,128)(2,1)}), bf16[1024,1024]{1,0:T(8,128)(2,1)}) %all-gather.8.cloned.1.call-update) | async-done | bytes 2097168 | tf_op jit(solution)/shard_map/all_gather | solution.py:104
  102.8 3.9 add_convert_fusion.1
  108.4 22.3 %while.27 = (s32[]{:T(128)}, bf16[2,512,4,64]{1,3,2,0:T(8,128)(2,1)}, f32[2,4,512]{2,1,0:T(4,128)S(1)}, s32[2]{0:T(128)S(1)}, s32[1024]{0:T(1024)S(1)}, /*index=...) while((s32[]{:T(128)}, ...), condition=%wide.region_12.13_spmd, body=%wide.region_9.12_spmd.sunk | while | flops 562690048 | bytes 35203332 | solution.py:137
  115.8 3.0 fusion.171
  126.9 3.0 fusion.171
  133.3 2.9 all_to_all.32
  138.1 4.1 all-to-all-start
  143.3 3.1 fusion.56
  146.4 3.2 copy.77
  149.6 7.6 %all-to-all-done = bf16[4,256,256]{1,2,0:T(8,128)(2,1)} async-done(((bf16[4,256,256]{1,2,0:T(8,128)(2,1)}), bf16[4,256,256]{1,2,0:T(8,128)(2,1)}, u32[]{:S(2)}, u32[]{:S(2)}) %all-to-all-start) | async-done | bytes 524320 | tf_op jit(solution)/shard_map/all_to_all | solution.py:139
  157.1 4.1 all-to-all-start.2
  165.5 5.5 all-to-all-done.2
  173.8 6.0 collective-permute-done
  183.7 44.5 %all-gather.10.cloned.1.call-done = bf16[1024,512]{1,0:T(8,128)(2,1)} async-done(((bf16[256,512]{1,0:T(8,128)(2,1)}), bf16[1024,512]{1,0:T(8,128)(2,1)}) %all-gather.10.cloned.1.call-update) | async-done | bytes 1048592 | tf_op jit(solution)/shard_map/all_gather | solution.py:202
  228.2 2.9 convolution_convert_fusion.4
  231.1 13.1 %collective-permute-done.1 = bf16[2,256,1024]{2,1,0:T(8,128)(2,1)} collective-permute-done((bf16[2,256,1024]{2,1,0:T(8,128)(2,1)}, bf16[2,256,1024]{2,1,0:T(8,128)(2,1)}, u32[]{:S(2)}, u32[]{:S(2)}) %collective-permute-start.1) | collective-permute-done | bytes 1048608 | tf_op jit(solution)/shard_map/ppermute | solution.py:21
  248.2 13.9 %convert_reduce_fusion = (f32[1024]{0:T(1024)}, bf16[1024,1024]{1,0:T(8,128)(2,1)S(1)}, f32[1024,1024]{1,0:T(8,128)}) fusion(f32[1024,1024]{1,0:T(8,128)S(1)} %fusion.107, f32[1024]{0:T(1024)S(1)} %convert_element_type.184, bf16[1024,1024]{1,0:T(8,128)(2,1)S(1)} %convolution_convert_fusion.4, bf16[1024,1024]{1,0:T(8,128)(2,1)S(1)} %copy-done), kind=kOutput, calls=%fused_computation.48 | convolution fusion | flops 2226125824 | bytes 14688256 | tf_op jit(solution)/shard_map/tc,fc->tf/dot_general | solution.py:214
  263.5 3.7 convolution_convert_fusion.3
  267.3 42.6 %reduce-scatter.8.cloned.1.call-done = bf16[256,1024]{1,0:T(8,128)(2,1)} async-done(((bf16[1024,1024]{1,0:T(8,128)(2,1)}), bf16[256,1024]{1,0:T(8,128)(2,1)}) %reduce-scatter.8.cloned.1.call-update) | async-done | bytes 524304 | tf_op jit(solution)/shard_map/reduce_scatter | solution.py:225
  317.2 3.1 convolution_convert_fusion.2
  320.5 4.6 multiply_convert_fusion.1
  331.1 4.4 fusion.108
  335.5 3.8 convolution_convert_fusion.1
  340.9 3.5 all-to-all-start.3
  344.4 3.1 add_convert_fusion.2
  347.6 6.1 convolution_convert_fusion
  353.7 5.1 all-to-all-done.3
  362.1 30.3 %while.28 = (s32[]{:T(128)}, f32[1024,4,64]{0,2,1:T(8,128)S(1)}, f32[1024,4,64]{0,2,1:T(8,128)}, bf16[2,512,4,64]{1,3,2,0:T(8,128)(2,1)}, s32[2]{0:T(128)S(1)}, ...) while((s32[]{:T(128)}, f32[1024,4,64]{0,2,1:T(8,128)S(1)}, ...), condition=%wide.region_21.22_spmd.clone, body=%wide.region_19.21_spmd.clone.sunk | while | flops 1375729664 | bytes 84740432 | solution.py:281
  369.3 3.3 multiply_reduce_fusion.3
  384.2 3.3 multiply_reduce_fusion.3
  396.7 4.6 fusion.50
  402.1 4.6 bitcast_convert_fusion
  406.8 2.8 convolution_convert_fusion.8
  409.6 3.7 all-to-all-start.1
  414.9 110.9 %all-reduce.7.cloned.1.call-done = bf16[1024,512]{1,0:T(8,128)(2,1)} async-done(((bf16[1024,512]{1,0:T(8,128)(2,1)}), bf16[1024,512]{1,0:T(8,128)(2,1)}) %all-reduce.7.cloned.1.call-update) | async-done | bytes 1048592 | tf_op jit(solution)/shard_map/psum | solution.py:309
  525.7 2.8 convert_element_type.221
  528.6 3.1 add_convert_fusion.3
  531.9 13.4 %all-reduce.2 = (f32[2,256]{1,0:T(2,128)}, f32[1024]{0:T(1024)}) all-reduce(f32[2,256]{1,0:T(2,128)S(1)} %pad_maximum_fusion.4, f32[1024]{0:T(1024)S(1)} %copy-done.53), channel_id=1, replica_groups=mesh['dp'=8,'mp'=4] {'dp'}, use_global_device_ids=true, to_apply=%region_35.36 | all-reduce | flops 1536 | bytes 12288 | tf_op jit(solution)/shard_map/psum | solution.py:310
  545.3 82.7 %all-reduce.9.cloned.1.call-done = (bf16[1024,3,256]{2,0,1:T(8,128)(2,1)}, bf16[1024,1024]{1,0:T(8,128)(2,1)}, bf16[1024,1024]{1,0:T(8,128)(2,1)}) async-done(((bf16[1024,3,256]{2,0,1:T(8,128)(2,1)}, bf16[1024,1024]{1,0:T(8,128)(2,1)}, bf16[1024,1024]{1,0:T(8,128)(2,1)}), (bf16[1024,3,256]{2,0,1:T(8,128)(2,1)}, bf16[1024,1024]{1,0:T(8,128)(2,1)}, bf16[1024,1024]{1,0:T(8,128)(2,1)})) %all-reduce.9.cloned.1.call-update) | async-done | bytes 5767184 | tf_op jit(solution)/shard_map/psum | solution.py:305
  628.1 3.5 convert_element_type.208
  636.6 13.9 %reduce-scatter.14.cloned.1.call-done = bf16[1,32,1024]{2,1,0:T(8,128)(2,1)} async-done(((bf16[4,32,1024]{2,1,0:T(8,128)(2,1)}), bf16[1,32,1024]{2,1,0:T(8,128)(2,1)}) %reduce-scatter.14.cloned.1.call-update) | async-done | bytes 65552 | tf_op jit(solution)/shard_map/reduce_scatter | solution.py:241
  650.4 10.1 %all-gather.2 = bf16[1,256,1024]{2,1,0:T(8,128)(2,1)S(1)} all-gather(bf16[1,32,1024]{2,1,0:T(8,128)(2,1)} %reduce-scatter.14.cloned.1.call-done), channel_id=4, replica_groups=mesh['dp'=8,'mp'=4] {'dp'}, dimensions={1}, use_global_device_ids=true | all-gather | bytes 589824 | tf_op jit(solution)/shard_map/all_gather | solution.py:242
  661.6 32.9 %reduce-scatter.10.cloned.1.call-done = bf16[256,1024]{1,0:T(8,128)(2,1)} async-done(((bf16[1024,1024]{1,0:T(8,128)(2,1)}), bf16[256,1024]{1,0:T(8,128)(2,1)}) %reduce-scatter.10.cloned.1.call-update) | async-done | bytes 524304 | tf_op jit(solution)/shard_map/reduce_scatter | solution.py:297
  697.9 3.6 fusion.98
  701.6 40.7 %all-reduce = (f32[1024]{0:T(1024)S(1)}, f32[1024]{0:T(1024)S(1)}, f32[1024]{0:T(1024)}, f32[1024]{0:T(1024)}, f32[1024]{0:T(1024)}, /*index=5*/f32[1024]{0:T(10...) all-reduce(f32[1024]{0:T(1024)S(1)} %get-tuple-element.176, ...), channel_id=1, replica_groups=mesh['dp'=8,'mp'=4] {'dp','mp'}, use_global_device_ids=true, to_apply=%region_28.29 | all-reduce | flops 9216 | bytes 73728 | tf_op jit(solution)/shard_map/psum | solution.py:311
  (272 shorter events, 100.6 us)
Async XLA Ops:
  7.2 241.0 %copy-start = (bf16[1024,1024]{1,0:T(8,128)(2,1)S(1)}, bf16[1024,1024]{1,0:T(8,128)(2,1)}, u32[]{:S(2)}) copy-start(bf16[1024,1024]{1,0:T(8,128)(2,1)} %param.39) | copy-start | bytes 6291460
  7.2 95.6 %all-gather.8.cloned.1.call-start = ((), (), s32[]{:S(2)}) async-start(), calls=%async_computation.9 | async-start | bytes 2621440 | tf_op jit(solution)/shard_map/all_gather | solution.py:104
  50.7 110.8 %copy-start.30 = (f32[1024]{0:T(1024)}, f32[1024]{0:T(1024)S(1)}, u32[]{:S(2)}) copy-start(f32[1024]{0:T(1024)S(1)} %get-tuple-element.261) | copy-start | bytes 12292
  50.7 110.8 %copy-start.32 = (f32[1024]{0:T(1024)}, f32[1024]{0:T(1024)S(1)}, u32[]{:S(2)}) copy-start(f32[1024]{0:T(1024)S(1)} %get-tuple-element.262) | copy-start | bytes 12292
  55.6 90.8 %all-gather.12.cloned.1.call-start = ((), (), s32[]{:S(2)}) async-start(), calls=%async_computation.17 | async-start | bytes 2359296 | tf_op jit(solution)/shard_map/all_gather | solution.py:49
  130.8 12.5 %copy-start.51 = (s32[1024]{0:T(1024)S(1)}, s32[1024]{0:T(1024)}, u32[]{:S(2)}) copy-start(s32[1024]{0:T(1024)} %param.28) | copy-start | bytes 12292
  138.1 19.0 %all-to-all-start = ((bf16[4,256,256]{1,2,0:T(8,128)(2,1)}), bf16[4,256,256]{1,2,0:T(8,128)(2,1)}, u32[]{:S(2)}, u32[]{:S(2)}) async-start(bf16[4,256,256]{1,2,0:T(8,128)(2,1)} %copy.76), calls=%async_computation | async-start | bytes 1048576 | tf_op jit(solution)/shard_map/all_to_all | solution.py:139
  143.3 27.8 %copy-start.56 = (s32[256]{0:T(256)}, s32[256]{0:T(256)S(1)}, u32[]{:S(2)}) copy-start(s32[256]{0:T(256)S(1)} %multiply_add_fusion.2) | copy-start | bytes 3076
  143.3 18.3 %copy-start.5 = (bf16[256,1024]{1,0:T(8,128)(2,1)S(1)}, bf16[256,1024]{1,0:T(8,128)(2,1)}, u32[]{:S(2)}) copy-start(bf16[256,1024]{1,0:T(8,128)(2,1)} %param.25) | copy-start | bytes 1572868
  143.3 18.3 %copy-start.38 = (f32[1024]{0:T(1024)S(1)}, f32[1024]{0:T(1024)}, u32[]{:S(2)}) copy-start(f32[1024]{0:T(1024)} %param.34) | copy-start | bytes 12292
  149.5 15.6 %copy-start.34 = (f32[1024]{0:T(1024)S(1)}, f32[1024]{0:T(1024)}, u32[]{:S(2)}) copy-start(f32[1024]{0:T(1024)} %param.35) | copy-start | bytes 12292
  149.5 15.6 %copy-start.39 = (f32[1024]{0:T(1024)S(1)}, f32[1024]{0:T(1024)}, u32[]{:S(2)}) copy-start(f32[1024]{0:T(1024)} %param.36) | copy-start | bytes 12292
  157.1 13.9 %all-to-all-start.2 = ((bf16[8,64,512]{2,1,0:T(8,128)(2,1)}), bf16[8,64,512]{2,1,0:T(8,128)(2,1)}, u32[]{:S(2)}, u32[]{:S(2)}) async-start(bf16[8,64,512]{2,1,0:T(8,128)(2,1)} %bitcast.170), calls=%async_computation.3 | async-start | bytes 1048576 | tf_op jit(solution)/shard_map/all_to_all | solution.py:179
  161.3 66.9 %all-gather.10.cloned.1.call-start = ((), (), s32[]{:S(2)}) async-start(), calls=%async_computation.11 | async-start | bytes 1310720 | tf_op jit(solution)/shard_map/all_gather | solution.py:202
  164.2 19.5 %copy-start.54 = (bf16[1024]{0:T(1024)(128)(2,1)S(1)}, bf16[1024]{0:T(1024)(128)(2,1)}, u32[]{:S(2)}) copy-start(bf16[1024]{0:T(1024)(128)(2,1)} %param.38) | copy-start | bytes 6148
  165.4 14.3 %collective-permute-start = (bf16[1,256,1024]{2,1,0:T(8,128)(2,1)S(1)}, bf16[1,256,1024]{2,1,0:T(8,128)(2,1)}, u32[]{:S(2)}, u32[]{:S(2)}) collective-permute-start(bf16[1,256,1024]{2,1,0:T(8,128)(2,1)S(1)} %fusion.86), channel_id=1, source_target_pairs={{0,1},{1,0},{2,3},{3,2},{4,5},{5,4},{6,7},{7,6},{8,9},{9,8},{10,11... | collective-permute-start | bytes 1572872 | tf_op jit(solution)/shard_map/ppermute | solution.py:21
  173.7 136.2 %reduce-scatter.8.cloned.1.call-start = ((), (), s32[]{:S(2)}) async-start(), calls=%async_computation.12 | async-start | bytes 2621440 | tf_op jit(solution)/shard_map/reduce_scatter | solution.py:225
  183.4 60.9 %collective-permute-start.1 = (bf16[2,256,1024]{2,1,0:T(8,128)(2,1)}, bf16[2,256,1024]{2,1,0:T(8,128)(2,1)}, u32[]{:S(2)}, u32[]{:S(2)}) collective-permute-start(bf16[2,256,1024]{2,1,0:T(8,128)(2,1)} %pad_maximum_fusion.2), channel_id=1, source_target_pairs={{0,2},{1,3},{2,0},{3,1},{4,6},{5,7},{6,4},{7,5},{8,10},{9,11},{10,... | collective-permute-start | bytes 3145736 | tf_op jit(solution)/shard_map/ppermute | solution.py:21
  228.2 16.0 %copy-start.14 = (bf16[1,256,1024]{2,1,0:T(8,128)(2,1)S(1)}, bf16[1,256,1024]{2,1,0:T(8,128)(2,1)}, u32[]{:S(2)}) copy-start(bf16[1,256,1024]{2,1,0:T(8,128)(2,1)} %copy-done.13) | copy-start | bytes 1572868
  231.1 17.1 %copy-start.63 = (bf16[1024,1024]{1,0:T(8,128)(2,1)}, bf16[1024,1024]{1,0:T(8,128)(2,1)S(1)}, u32[]{:S(2)}) copy-start(bf16[1024,1024]{1,0:T(8,128)(2,1)S(1)} %convolution_convert_fusion.4) | copy-start | bytes 6291460
  231.1 14.7 %copy-start.58 = (bf16[1024,1024]{1,0:T(8,128)(2,1)S(1)}, bf16[1024,1024]{1,0:T(8,128)(2,1)}, u32[]{:S(2)}) copy-start(bf16[1024,1024]{1,0:T(8,128)(2,1)} %param.37) | copy-start | bytes 6291460
  248.2 14.0 %copy-start.15 = (f32[1024,1024]{1,0:T(8,128)}, f32[1024,1024]{1,0:T(8,128)S(1)}, u32[]{:S(2)}) copy-start(f32[1024,1024]{1,0:T(8,128)S(1)} %fusion.107) | copy-start | bytes 12582916
  267.2 47.9 %copy-start.16 = (bf16[256,512]{1,0:T(8,128)(2,1)S(1)}, bf16[256,512]{1,0:T(8,128)(2,1)}, u32[]{:S(2)}) copy-start(bf16[256,512]{1,0:T(8,128)(2,1)} %get-tuple-element.258) | copy-start | bytes 786436
  267.2 134.1 %reduce-scatter.12.cloned.1.call-start = ((), (), s32[]{:S(2)}) async-start(), calls=%async_computation.14 | async-start | bytes 2359296 | tf_op jit(solution)/shard_map/reduce_scatter | solution.py:240
  320.3 86.5 %reduce-scatter.6.cloned.1.call-start = ((), (), s32[]{:S(2)}) async-start(), calls=%async_computation.10 | async-start | bytes 1310720 | tf_op jit(solution)/shard_map/reduce_scatter | solution.py:150
  340.9 17.9 %all-to-all-start.3 = ((bf16[256,4,256]{2,0,1:T(8,128)(2,1)}), bf16[256,4,256]{2,0,1:T(8,128)(2,1)S(1)}, u32[]{:S(2)}, u32[]{:S(2)}) async-start(bf16[256,4,256]{2,0,1:T(8,128)(2,1)} %bitcast.167), calls=%async_computation.5 | async-start | bytes 1048576 | tf_op jit(solution)/shard_map/all_to_all | solution.py:243
  344.4 181.4 %all-reduce.7.cloned.1.call-start = ((), (), s32[]{:S(2)}) async-start(), calls=%async_computation.16 | async-start | bytes 2097152 | tf_op jit(solution)/shard_map/psum | solution.py:309
  347.5 14.6 %copy-start.8 = (bf16[1024,4,64]{0,2,1:T(8,128)(2,1)S(1)}, bf16[1024,4,64]{0,2,1:T(8,128)(2,1)}, u32[]{:S(2)}) copy-start(bf16[1024,4,64]{0,2,1:T(8,128)(2,1)} %copy-done.7) | copy-start | bytes 1572868
  347.5 14.5 %copy-start.10 = (bf16[1024,4,64]{0,2,1:T(8,128)(2,1)S(1)}, bf16[1024,4,64]{0,2,1:T(8,128)(2,1)}, u32[]{:S(2)}) copy-start(bf16[1024,4,64]{0,2,1:T(8,128)(2,1)} %get-tuple-element.487) | copy-start | bytes 1572868
  347.5 280.5 %all-reduce.9.cloned.1.call-start = ((), (), s32[]{:S(2)}) async-start(), calls=%async_computation.18 | async-start | bytes 11534336 | tf_op jit(solution)/shard_map/psum | solution.py:305
  401.3 249.2 %reduce-scatter.14.cloned.1.call-start = ((), (), s32[]{:S(2)}) async-start(), calls=%async_computation.15 | async-start | bytes 327680 | tf_op jit(solution)/shard_map/reduce_scatter | solution.py:241
  402.1 292.4 %reduce-scatter.10.cloned.1.call-start = ((), (), s32[]{:S(2)}) async-start(), calls=%async_computation.13 | async-start | bytes 2621440 | tf_op jit(solution)/shard_map/reduce_scatter | solution.py:297
  406.8 121.8 %copy-start.61 = (f32[512]{0:T(512)S(1)}, f32[512]{0:T(512)}, u32[]{:S(2)}) copy-start(f32[512]{0:T(512)} %param.43) | copy-start | bytes 6148
  409.6 119.0 %all-to-all-start.1 = ((bf16[8,64,512]{2,1,0:T(8,128)(2,1)}), bf16[8,64,512]{2,1,0:T(8,128)(2,1)S(1)}, u32[]{:S(2)}, u32[]{:S(2)}) async-start(bf16[8,64,512]{2,1,0:T(8,128)(2,1)} %bitcast.21), calls=%async_computation.2 | async-start | bytes 1048576 | tf_op jit(solution)/shard_map/all_to_all | solution.py:172
  414.8 117.1 %copy-start.53 = (f32[1024]{0:T(1024)S(1)}, f32[1024]{0:T(1024)}, u32[]{:S(2)}) copy-start(f32[1024]{0:T(1024)} %get-tuple-element.237) | copy-start | bytes 12292
  634.0 60.4 %copy-start.6 = (bf16[256,1024]{1,0:T(8,128)(2,1)S(1)}, bf16[256,1024]{1,0:T(8,128)(2,1)}, u32[]{:S(2)}) copy-start(bf16[256,1024]{1,0:T(8,128)(2,1)} %param.25) | copy-start | bytes 1572868
  634.0 60.4 %copy-start.31 = (f32[1024]{0:T(1024)S(1)}, f32[1024]{0:T(1024)}, u32[]{:S(2)}) copy-start(f32[1024]{0:T(1024)} %copy-done.30) | copy-start | bytes 12292
  634.0 60.4 %copy-start.33 = (f32[1024]{0:T(1024)S(1)}, f32[1024]{0:T(1024)}, u32[]{:S(2)}) copy-start(f32[1024]{0:T(1024)} %copy-done.32) | copy-start | bytes 12292
  634.0 60.4 %copy-start.35 = (f32[1024]{0:T(1024)S(1)}, f32[1024]{0:T(1024)}, u32[]{:S(2)}) copy-start(f32[1024]{0:T(1024)} %param.29) | copy-start | bytes 12292
  634.0 60.4 %copy-start.37 = (f32[256]{0:T(256)S(1)}, f32[256]{0:T(256)}, u32[]{:S(2)}) copy-start(f32[256]{0:T(256)} %copy-done.36) | copy-start | bytes 3076
  634.1 62.1 %copy-start.46 = (f32[256]{0:T(256)S(1)}, f32[256]{0:T(256)}, u32[]{:S(2)}) copy-start(f32[256]{0:T(256)} %copy-done.45) | copy-start | bytes 3076
  634.1 62.1 %copy-start.44 = (f32[256]{0:T(256)S(1)}, f32[256]{0:T(256)}, u32[]{:S(2)}) copy-start(f32[256]{0:T(256)} %copy-done.43) | copy-start | bytes 3076
  634.1 63.8 %copy-start.49 = (f32[256]{0:T(256)S(1)}, f32[256]{0:T(256)}, u32[]{:S(2)}) copy-start(f32[256]{0:T(256)} %copy-done.48) | copy-start | bytes 3076
  636.6 65.0 %copy-start.40 = (f32[1024]{0:T(1024)S(1)}, f32[1024]{0:T(1024)}, u32[]{:S(2)}) copy-start(f32[1024]{0:T(1024)} %get-tuple-element.171) | copy-start | bytes 12292
  636.6 65.0 %copy-start.41 = (f32[1024]{0:T(1024)S(1)}, f32[1024]{0:T(1024)}, u32[]{:S(2)}) copy-start(f32[1024]{0:T(1024)} %get-tuple-element.177) | copy-start | bytes 12292
  636.6 65.0 %copy-start.42 = (f32[1024]{0:T(1024)S(1)}, f32[1024]{0:T(1024)}, u32[]{:S(2)}) copy-start(f32[1024]{0:T(1024)} %get-tuple-element.240) | copy-start | bytes 12292
  636.6 65.0 %copy-start.55 = (f32[512]{0:T(512)S(1)}, f32[512]{0:T(512)}, u32[]{:S(2)}) copy-start(f32[512]{0:T(512)} %get-tuple-element.257) | copy-start | bytes 6148
  694.5 50.2 %copy-start.1 = (bf16[1024,1024]{1,0:T(8,128)(2,1)S(1)}, bf16[1024,1024]{1,0:T(8,128)(2,1)}, u32[]{:S(2)}) copy-start(bf16[1024,1024]{1,0:T(8,128)(2,1)} %param.39) | copy-start | bytes 6291460
  (41 other events, 133.7 us)
Sparse Core Ops, SparseCore 0:
  55.7 47.0 all-gather.7
  104.6 26.8 all-gather.11
  173.8 54.3 all-gather.9
  267.4 42.4 reduce-scatter.7
  320.4 40.2 reduce-scatter.11
  363.4 27.3 reduce-scatter.5
  396.5 129.1 all-reduce.6
  530.5 97.5 all-reduce.8
  630.3 20.0 reduce-scatter.13
  652.6 41.8 reduce-scatter.9
